TPU v7x, 128 devices: a whole 4x4x4 slice. The times are simulated.
128 devices in a mesh: cfg: 2 (over core), lat: 4 (over x), seq: 16 (over z, y).
Axes of the slice: x: 4, y: 4, z: 4, core: 2. Of those that a mesh axis runs over, the one named last changes fastest.
Arguments:
- latents: float32 [24, 1024, 16], P('lat', 'seq'), may hold values from -6 to 6
- timesteps: int32 [24], P('lat'), may hold values from 0 to 999
- labels: int32 [24], P('lat'), may hold values from 0 to 999
- guidance: float32 [1], replicated, may hold values from 1.5 to 4
- keep_coef: float32 [24], P('lat'), may hold values from 0.8 to 1.2
- noise_coef: float32 [24], P('lat'), may hold values from -0.6 to -0.2
- w_patch: bfloat16 [16, 1152], replicated, may hold values from -1.5 to 1.5
- label_table: bfloat16 [1001, 1152], replicated, may hold values from -6 to 6
- w_time1: bfloat16 [256, 1152], P(None, 'lat'), may hold values from -0.375 to 0.375
- w_time2: bfloat16 [1152, 1152], P(None, 'lat'), may hold values from -0.1875 to 0.1875
- ada_weight: bfloat16 [1152, 9216], P(None, 'seq'), may hold values from -0.1875 to 0.1875
- w_qkv: bfloat16 [1152, 3456], P(None, 'seq'), may hold values from -2.9168155 to 2.9168155
- w_proj: bfloat16 [1152, 1152], P(None, 'seq'), may hold values from -0.1875 to 0.1875
- w_fc1: bfloat16 [1152, 4608], P(None, 'seq'), may hold values from -0.1875 to 0.1875
- w_fc2: bfloat16 [4608, 1152], P('seq'), may hold values from -0.09375 to 0.09375
- w_out: bfloat16 [1152, 16], replicated, may hold values from -0.1875 to 0.1875
Outputs:
- next_latents: float32 [24, 1024, 16], P('lat', 'seq', 'cfg')
All inputs are finite; a program needn't handle non-finite values.
Results may differ from a plain program's by a relative error of at most 0.009.
Values may be sent and summed in bfloat16 or wider, within the bound.
A program may use at most 192 MiB of HBM per device.

v0:
```python
import math
import jax
import jax.numpy as jnp
from jax import lax
from jax.sharding import PartitionSpec as P

D = 1152
HEADS = 16
HEAD_DIM = 72
CLASSES = 1000
FREQ = 256
GRID = 32


def swapped(value, axis, stride):
    mask = 2**stride
    pairs = [(source, source ^ mask) for source in range(lax.axis_size(axis))]
    return lax.ppermute(value, axis, pairs)


def layer_norm(values):
    average = jnp.mean(values, axis=-1, keepdims=True)
    centered = values - average
    spread = jnp.mean(centered * centered, axis=-1, keepdims=True)
    return centered * lax.rsqrt(spread + 1e-06)


def modulate(values, shifted, scaled):
    return layer_norm(values) * (1.0 + scaled[:, None, :]) + shifted[:, None, :]


def time_waves(timesteps):
    half_count = FREQ // 2
    frequency = jnp.exp(-math.log(10000.0) * jnp.arange(half_count, dtype=jnp.float32) / half_count)
    angles = timesteps.astype(jnp.float32)[:, None] * frequency[None, :]
    return jnp.concatenate([jnp.cos(angles), jnp.sin(angles)], axis=-1)


def grid_waves(positions):
    quarter = D // 4
    frequency = jnp.exp(-math.log(10000.0) * jnp.arange(quarter, dtype=jnp.float32) / quarter)
    column = (positions % GRID).astype(jnp.float32)[:, None] * frequency[None, :]
    row_angle = (positions // GRID).astype(jnp.float32)[:, None] * frequency[None, :]
    return jnp.concatenate(
        [jnp.sin(column), jnp.cos(column), jnp.sin(row_angle), jnp.cos(row_angle)], axis=-1
    )


def condition(timesteps, classes, label_table, w_time1, w_time2):
    waves = time_waves(timesteps).astype(jnp.bfloat16)
    hidden_time = jax.nn.silu(jnp.dot(waves, w_time1, preferred_element_type=jnp.float32)).astype(
        jnp.bfloat16
    )
    time_vector = jnp.dot(hidden_time, w_time2, preferred_element_type=jnp.float32)
    onehot = (classes[:, None] == jnp.arange(CLASSES + 1, dtype=jnp.int32)[None, :]).astype(
        jnp.bfloat16
    )
    return time_vector + jnp.dot(onehot, label_table, preferred_element_type=jnp.float32)


def shards(
    latents,
    timesteps,
    labels,
    guidance,
    keep_coef,
    noise_coef,
    w_patch,
    label_table,
    w_time1,
    w_time2,
    ada_weight,
    w_qkv,
    w_proj,
    w_fc1,
    w_fc2,
    w_out,
):
    lat_count, tok_count, channels = latents.shape
    model_width = w_patch.shape[1]
    side_index = lax.axis_index("cfg")
    classes = jnp.where(side_index == 0, labels, CLASSES)
    time_first, time_second = (
        lax.all_gather(w_time1, "lat", axis=1, tiled=True),
        lax.all_gather(w_time2, "lat", axis=1, tiled=True),
    )
    conditioning = condition(timesteps, classes, label_table, time_first, time_second)
    own_columns = jnp.dot(
        jax.nn.silu(conditioning).astype(jnp.bfloat16),
        ada_weight,
        preferred_element_type=jnp.float32,
    )
    modulation = lax.all_gather(own_columns, "seq", axis=1, tiled=True)
    pieces = [
        modulation[:, number * model_width : (number + 1) * model_width] for number in range(8)
    ]
    positions = lax.axis_index("seq") * tok_count + jnp.arange(tok_count, dtype=jnp.int32)
    state = jnp.dot(
        latents.reshape(-1, channels).astype(jnp.bfloat16),
        w_patch,
        preferred_element_type=jnp.float32,
    )
    state = state.reshape(lat_count, tok_count, model_width) + grid_waves(positions)[None]
    qkv_full, proj_full = (
        lax.all_gather(w_qkv, "seq", axis=1, tiled=True),
        lax.all_gather(w_proj, "seq", axis=1, tiled=True),
    )
    normed = modulate(state, pieces[0], pieces[1]).astype(jnp.bfloat16).reshape(-1, model_width)
    triple = jnp.dot(normed, qkv_full, preferred_element_type=jnp.float32).astype(jnp.bfloat16)
    queries = triple[:, :model_width].reshape(lat_count, tok_count, HEADS, HEAD_DIM)
    keys_own = triple[:, model_width : 2 * model_width].reshape(lat_count, tok_count, model_width)
    values_own = triple[:, 2 * model_width :].reshape(lat_count, tok_count, model_width)
    factor = 1.0 / math.sqrt(HEAD_DIM)
    row_best = jnp.full((lat_count, HEADS, tok_count), -1e30, jnp.float32)
    keys_part = lax.all_gather(keys_own, "seq", axis=1, tiled=True)
    values_part = lax.all_gather(values_own, "seq", axis=1, tiled=True)
    key_count = keys_part.shape[1]
    keys_heads = keys_part.reshape(lat_count, key_count, HEADS, HEAD_DIM)
    values_heads = values_part.reshape(lat_count, key_count, HEADS, HEAD_DIM)
    scores = (
        jnp.einsum("lqhd,lkhd->lhqk", queries, keys_heads, preferred_element_type=jnp.float32)
        * factor
    )
    raised = jnp.maximum(row_best, jnp.max(scores, axis=-1))
    exponent = jnp.exp(scores - raised[..., None])
    row_sums = jnp.sum(exponent, axis=-1)
    weighted = jnp.einsum(
        "lhqk,lkhd->lhqd",
        exponent.astype(jnp.bfloat16),
        values_heads,
        preferred_element_type=jnp.float32,
    )
    row_best, row_sums, weighted = (raised, row_sums, weighted)
    attended = (
        (weighted / row_sums[..., None])
        .transpose(0, 2, 1, 3)
        .reshape(-1, model_width)
        .astype(jnp.bfloat16)
    )
    projected = jnp.dot(attended, proj_full, preferred_element_type=jnp.float32)
    state = state + pieces[2][:, None, :] * projected.reshape(lat_count, tok_count, model_width)
    normed = modulate(state, pieces[3], pieces[4]).astype(jnp.bfloat16).reshape(-1, model_width)
    fc1_full, fc2_full = (
        lax.all_gather(w_fc1, "seq", axis=1, tiled=True),
        lax.all_gather(w_fc2, "seq", axis=0, tiled=True),
    )
    hidden = jax.nn.gelu(
        jnp.dot(normed, fc1_full, preferred_element_type=jnp.float32), approximate=True
    ).astype(jnp.bfloat16)
    mlp_out = jnp.dot(hidden, fc2_full, preferred_element_type=jnp.float32)
    state = state + pieces[5][:, None, :] * mlp_out.reshape(lat_count, tok_count, model_width)
    final = modulate(state, pieces[6], pieces[7]).astype(jnp.bfloat16).reshape(-1, model_width)
    noise_own = jnp.dot(final, w_out, preferred_element_type=jnp.float32).reshape(
        lat_count, tok_count, channels
    )
    half_width = channels // 2
    own_latent = lax.dynamic_slice_in_dim(latents, side_index * half_width, half_width, 2)
    partner = swapped(noise_own, "cfg", 0)
    cond_noise = jnp.where(side_index == 0, noise_own, partner)
    free_noise = jnp.where(side_index == 0, partner, noise_own)
    combined = free_noise + guidance[0] * (cond_noise - free_noise)
    guided = lax.dynamic_slice_in_dim(combined, side_index * half_width, half_width, 2)
    return keep_coef[:, None, None] * own_latent + noise_coef[:, None, None] * guided


def solution(mesh):
    return jax.shard_map(
        shards,
        mesh=mesh,
        in_specs=(
            P("lat", "seq", None),
            P("lat"),
            P("lat"),
            P(),
            P("lat"),
            P("lat"),
            P(),
            P(),
            P(None, "lat"),
            P(None, "lat"),
            P(None, "seq"),
            P(None, "seq"),
            P(None, "seq"),
            P(None, "seq"),
            P("seq", None),
            P(),
        ),
        out_specs=P("lat", "seq", "cfg"),
        check_vma=False,
    )
```

profile of v0, /device:TPU:1, one launch (start us, length us, event | category | flops | bytes accessed | tf_op | source)
XLA Modules:
  0.0 571.2 jit_solution(164010904563712114)
XLA Ops:
  9.7 1.3 fusion.61
  12.6 12.5 %all_gather.27 = bf16[256,1152]{0,1:T(8,128)(2,1)S(1)} all-gather(bf16[256,288]{0,1:T(8,128)(2,1)S(1)} %copy-done.5), channel_id=1, replica_groups=mesh['cfg'=2,'lat'=4,'seq'=16] {'lat'}, dimensions={1}, use_global_device_ids=true | all-gather | bytes 737280 | tf_op jit(solution)/shard_map/all_gather | solution.py:84
  25.2 23.4 %all-gather.9.cloned.1.call-done = bf16[1152,1152]{0,1:T(8,128)(2,1)} async-done(((bf16[1152,288]{0,1:T(8,128)(2,1)}), bf16[1152,1152]{0,1:T(8,128)(2,1)}) %all-gather.9.cloned.1.call-update) | async-done | bytes 2654224 | tf_op jit(solution)/shard_map/all_gather | solution.py:85
  48.6 2.7 fusion.31
  51.3 2.1 convolution_bitcast_fusion
  53.5 21.0 %all-gather = f32[16,576,6]{1,2,0:T(8,128)S(1)} all-gather(f32[1,576,6]{1,2,0:T(8,128)S(1)} %convolution_bitcast_fusion), channel_id=1, replica_groups=mesh['cfg'=2,'lat'=4,'seq'=16] {'seq'}, dimensions={0}, use_global_device_ids=true | all-gather | bytes 235008 | tf_op jit(solution)/shard_map/all_gather | solution.py:93
  75.1 45.3 %all-gather.11.cloned.1.call-done = bf16[1152,3456]{0,1:T(8,128)(2,1)} async-done(((bf16[1152,216]{0,1:T(8,128)(2,1)}), bf16[1152,3456]{0,1:T(8,128)(2,1)}) %all-gather.11.cloned.1.call-update) | async-done | bytes 7962640 | tf_op jit(solution)/shard_map/all_gather | solution.py:105
  120.4 8.3 %convolution_convert_fusion = bf16[384,3456]{1,0:T(8,128)(2,1)S(1)} fusion(bf16[384,1152]{1,0:T(8,128)(2,1)S(1)} %bitcast.55, bf16[1152,3456]{0,1:T(8,128)(2,1)} %all-gather.11.cloned.1.call-done), kind=kOutput, calls=%fused_computation.16 | convolution fusion | flops 3058974720 | bytes 11501568 | tf_op jit(solution)/shard_map/dot_general | solution.py:109
  128.7 1.5 fusion.60
  132.6 3.6 reshape.137
  136.3 91.6 %all-gather.13.cloned.1.call-done = bf16[6,1024,1152]{2,1,0:T(8,128)(2,1)} async-done(((bf16[6,64,1152]{2,1,0:T(8,128)(2,1)}), bf16[6,1024,1152]{2,1,0:T(8,128)(2,1)}) %all-gather.13.cloned.1.call-update) | async-done | bytes 14155792 | tf_op jit(solution)/shard_map/all_gather | solution.py:115
  227.9 18.7 %copy.27 = bf16[6,1024,1152]{1,2,0:T(8,128)(2,1)} copy(bf16[6,1024,1152]{2,1,0:T(8,128)(2,1)} %all-gather.13.cloned.1.call-done) | data formatting | bytes 28311552 | tf_op jit(solution)/shard_map/all_gather | solution.py:115
  246.7 80.9 %all-gather.15.cloned.1.call-done = bf16[6,1024,1152]{2,1,0:T(8,128)(2,1)} async-done(((bf16[6,64,1152]{2,1,0:T(8,128)(2,1)}), bf16[6,1024,1152]{2,1,0:T(8,128)(2,1)}) %all-gather.15.cloned.1.call-update) | async-done | bytes 14155792 | tf_op jit(solution)/shard_map/all_gather | solution.py:116
  327.6 18.7 %copy.29 = bf16[6,1024,1152]{1,2,0:T(8,128)(2,1)} copy(bf16[6,1024,1152]{2,1,0:T(8,128)(2,1)} %all-gather.15.cloned.1.call-done) | data formatting | bytes 28311552 | tf_op jit(solution)/shard_map/all_gather | solution.py:116
  346.3 18.5 %multiply_reduce_fusion = (f32[6,16,64]{2,1,0:T(8,128)S(1)}, f32[6,16,64,1024]{3,2,1,0:T(8,128)}) fusion(bf16[6,1024,16,72]{1,3,2,0:T(8,128)(2,1)} %bitcast.48, bf16[6,64,16,72]{3,2,1,0:T(8,128)(2,1)} %reshape.137), kind=kOutput, calls=%fused_computation.1 | convolution fusion | flops 918546432 | bytes 40230912 | tf_op jit(solution)/shard_map/lqhd,lkhd->lhqk/dot_general | solution.py:121
  364.8 11.2 %fusion = f32[6,16,64]{2,1,0:T(8,128)S(1)} fusion(f32[6,16,64,1024]{3,2,1,0:T(8,128)} %get-tuple-element.29, f32[6,16,64]{2,1,0:T(8,128)S(1)} %broadcast_maximum_fusion), kind=kLoop, calls=%fused_computation.2 | loop fusion | flops 18868224 | bytes 25214976 | tf_op jit(solution)/shard_map/reduce_sum | solution.py:126
  376.0 14.7 %fusion.20 = bf16[6,64,16,72]{3,1,2,0:T(8,128)(2,1)S(1)} fusion(bf16[6,1024,16,72]{1,3,2,0:T(8,128)(2,1)} %bitcast.49, f32[6,16,64,1024]{3,2,1,0:T(8,128)} %get-tuple-element.29, f32[6,16,64]{2,1,0:T(8,128)S(1)} %broadcast_maximum_fusion, f32[6,64,16]{1,2,0:T(8,128)S(1)} %bitcast.56), kind=kOutput, calls=%fused_computation.25 | convolution fusion | flops 925728768 | bytes 40255488 | tf_op jit(solution)/shard_map/lhqk,lkhd->lhqd/dot_general | solution.py:127
  390.8 2.2 copy.30
  393.0 3.2 convert_element_type.64
  396.2 3.3 fusion.62
  401.3 56.8 %all-gather.19.cloned.1.call-done = bf16[1152,4608]{0,1:T(8,128)(2,1)} async-done(((bf16[1152,288]{0,1:T(8,128)(2,1)}), bf16[1152,4608]{0,1:T(8,128)(2,1)}) %all-gather.19.cloned.1.call-update) | async-done | bytes 10616848 | tf_op jit(solution)/shard_map/all_gather | solution.py:144
  458.1 82.9 %all-gather.21.cloned.1.call-done = bf16[4608,1152]{1,0:T(8,128)(2,1)} async-done(((bf16[288,1152]{1,0:T(8,128)(2,1)}), bf16[4608,1152]{1,0:T(8,128)(2,1)}) %all-gather.21.cloned.1.call-update) | async-done | bytes 10616848 | tf_op jit(solution)/shard_map/all_gather | solution.py:145
  540.9 17.6 %fusion.14 = f32[384,1152]{1,0:T(8,128)} fusion(bf16[4608,1152]{1,0:T(8,128)(2,1)} %all-gather.21.cloned.1.call-done, bf16[384,1152]{1,0:T(8,128)(2,1)S(1)} %bitcast.54, bf16[1152,4608]{0,1:T(8,128)(2,1)} %all-gather.19.cloned.1.call-done), kind=kOutput, calls=%fused_computation.17 | convolution fusion | flops 8169652224 | bytes 23887872 | tf_op jit(solution)/shard_map/dot_general | solution.py:150
  558.6 2.5 fusion.59
  (64 shorter events, 12.1 us)
Async XLA Ops:
  6.5 44.8 %copy-start = (bf16[1001,1152]{1,0:T(8,128)(2,1)S(1)}, bf16[1001,1152]{1,0:T(8,128)(2,1)}, u32[]{:S(2)}) copy-start(bf16[1001,1152]{1,0:T(8,128)(2,1)} %param.23) | copy-start | bytes 6918916
  6.5 3.2 copy-start.6
  6.5 42.0 %all-gather.9.cloned.1.call-start = ((), (), s32[]{:S(2)}) async-start(), calls=%async_computation | async-start | bytes 3317760 | tf_op jit(solution)/shard_map/all_gather | solution.py:85
  7.3 113.1 %all-gather.11.cloned.1.call-start = ((), (), s32[]{:S(2)}) async-start(), calls=%async_computation.1 | async-start | bytes 8460288 | tf_op jit(solution)/shard_map/all_gather | solution.py:105
  8.0 219.9 %all-gather.13.cloned.1.call-start = ((), (), s32[]{:S(2)}) async-start(), calls=%async_computation.2 | async-start | bytes 15040512 | tf_op jit(solution)/shard_map/all_gather | solution.py:115
  9.5 3.0 copy-start.5
  9.7 15.3 %copy-start.10 = (s32[6]{0:T(128)S(1)}, s32[6]{0:T(128)}, u32[]{:S(2)}) copy-start(s32[6]{0:T(128)} %param.18) | copy-start | bytes 76
  11.0 1.2 copy-start.2
  53.5 21.2 %copy-start.3 = (f32[6,64,1152]{2,1,0:T(8,128)S(1)}, f32[6,64,1152]{2,1,0:T(8,128)}, u32[]{:S(2)}) copy-start(f32[6,64,1152]{2,1,0:T(8,128)} %copy-done.2) | copy-start | bytes 5308420
  130.2 197.4 %all-gather.15.cloned.1.call-start = ((), (), s32[]{:S(2)}) async-start(), calls=%async_computation.3 | async-start | bytes 15040512 | tf_op jit(solution)/shard_map/all_gather | solution.py:116
  130.7 265.5 %all-gather.17.cloned.1.call-start = ((), (), s32[]{:S(2)}) async-start(), calls=%async_computation.4 | async-start | bytes 2820096 | tf_op jit(solution)/shard_map/all_gather | solution.py:106
  131.3 326.7 %all-gather.19.cloned.1.call-start = ((), (), s32[]{:S(2)}) async-start(), calls=%async_computation.5 | async-start | bytes 11280384 | tf_op jit(solution)/shard_map/all_gather | solution.py:144
  131.9 409.0 %all-gather.21.cloned.1.call-start = ((), (), s32[]{:S(2)}) async-start(), calls=%async_computation.6 | async-start | bytes 11280384 | tf_op jit(solution)/shard_map/all_gather | solution.py:145
  399.6 1.3 copy-start.4
  558.6 2.9 copy-start.9
  558.6 5.7 %copy-start.1 = (bf16[1001,1152]{1,0:T(8,128)(2,1)S(1)}, bf16[1001,1152]{1,0:T(8,128)(2,1)}, u32[]{:S(2)}) copy-start(bf16[1001,1152]{1,0:T(8,128)(2,1)} %param.23) | copy-start | bytes 6918916
  561.1 2.5 copy-start.7
  561.1 2.5 copy-start.8
  562.0 1.6 collective-permute-start
Sparse Core Ops, SparseCore 0:
  9.0 39.5 all-gather.8
  50.7 69.6 all-gather.10
  130.3 97.5 all-gather.12
  229.9 97.6 all-gather.14
  329.6 45.8 all-gather.16
  377.4 80.5 all-gather.18
  460.2 80.6 all-gather.20
where the time goes:
time: 573 us; the launch traced here: 571 us
  waiting for transfers between devices  385 us (67%)
  matrix products  69.3 us (12%)
  local copies, waits for them, and re-layouts  50.5 us (9%)
  blocking collectives  33.4 us (6%)
  other arithmetic  17.8 us (3%)
  between operations  14.4 us (3%)
    all_gather x1, waiting for transfers between devices, shards(): keys_part = lax.all_gather(keys_own, 'seq', axis=1, tiled=True)  91.6 us
    all_gather x1, waiting for transfers between devices, shards(): lax.all_gather(w_fc2, 'seq', axis=0, tiled=True)  82.9 us
    all_gather x1, waiting for transfers between devices, shards(): values_part = lax.all_gather(values_own, 'seq', axis=1, tiled=True)  80.9 us
    all_gather x1, waiting for transfers between devices, shards(): lax.all_gather(w_fc1, 'seq', axis=1, tiled=True)  56.8 us
    all_gather x1, waiting for transfers between devices, shards(): lax.all_gather(w_qkv, 'seq', axis=1, tiled=True)  45.3 us
    all_gather x1, waiting for transfers between devices, shards(): lax.all_gather(w_time2, 'lat', axis=1, tiled=True)  23.4 us
    all_gather x1, blocking collectives, shards(): modulation = lax.all_gather(own_columns, 'seq', axis=1, tiled=True)  21 us
    all_gather x1, local copies, waits for them, and re-layouts, shards(): keys_part = lax.all_gather(keys_own, 'seq', axis=1, tiled=True)  18.7 us
  transfers between devices with their start and end apart: 8, of which 7 were waited for; matrix products, arithmetic and copies ran while one was open for 18% of the time, Pallas kernels for 0%

commit v1 on v0

--- a/solution.py
+++ b/solution.py
@@ -82,7 +82,9 @@
     classes = jnp.where(side_index == 0, labels, CLASSES)
     time_first, time_second = (
         lax.all_gather(w_time1, "lat", axis=1, tiled=True),
-        lax.all_gather(w_time2, "lat", axis=1, tiled=True),
+        jnp.concatenate(
+            lax.all_to_all(jnp.stack([w_time2] * lax.axis_size("lat")), "lat", 0, 0), axis=1
+        ),
     )
     conditioning = condition(timesteps, classes, label_table, time_first, time_second)
     own_columns = jnp.dot(

time: 573 us -> 539 us (0.941)
  waiting for transfers between devices: 385 us -> 320 us
  blocking collectives: 33.4 us -> 58.5 us
    all_gather x1, waiting for transfers between devices: 45.3 us -> 0.65 us  [shards(): lax.all_gather(w_qkv, 'seq', axis=1, tiled=True)]
    all_gather x1 -> x0, waiting for transfers between devices: 23.4 us -> none  [shards(): lax.all_gather(w_time2, 'lat', axis=1, tiled=True)]
    all_gather x1, blocking collectives: 12.5 us -> 34.9 us  [shards(): lax.all_gather(w_time1, 'lat', axis=1, tiled=True)]
  transfers between devices with their start and end apart: 8 -> 8, of which waited for: 7 -> 6; matrix products, arithmetic and copies ran while one was open for 18% -> 20% of each run, Pallas kernels for 0% -> 0%
where the time goes in v1:
time: 539 us; the launch traced here: 538 us
  waiting for transfers between devices  320 us (59%)
  matrix products  68.6 us (13%)
  blocking collectives  58.5 us (11%)
  local copies, waits for them, and re-layouts  53.3 us (10%)
  other arithmetic  17.2 us (3%)
  between operations  14.4 us (3%)
  starting transfers between devices  6.02 us (1%)
    all_gather x1, waiting for transfers between devices, shards(): keys_part = lax.all_gather(keys_own, 'seq', axis=1, tiled=True)  95.5 us
    all_gather x1, waiting for transfers between devices, shards(): lax.all_gather(w_fc2, 'seq', axis=0, tiled=True)  82.7 us
    all_gather x1, waiting for transfers between devices, shards(): values_part = lax.all_gather(values_own, 'seq', axis=1, tiled=True)  81.1 us
    all_gather x1, waiting for transfers between devices, shards(): lax.all_gather(w_fc1, 'seq', axis=1, tiled=True)  56.8 us
    all_gather x1, blocking collectives, shards(): lax.all_gather(w_time1, 'lat', axis=1, tiled=True)  34.9 us
    all_gather x1, blocking collectives, shards(): modulation = lax.all_gather(own_columns, 'seq', axis=1, tiled=True)  23.6 us
    all_gather x1, local copies, waits for them, and re-layouts, shards(): keys_part = lax.all_gather(keys_own, 'seq', axis=1, tiled=True)  18.7 us
    all_gather x1, local copies, waits for them, and re-layouts, shards(): values_part = lax.all_gather(values_own, 'seq', axis=1, tiled=True)  18.7 us
  transfers between devices with their start and end apart: 8, of which 6 were waited for; matrix products, arithmetic and copies ran while one was open for 20% of the time, Pallas kernels for 0%

profile of v1, /device:TPU:1, one launch (start us, length us, event | category | flops | bytes accessed | tf_op | source)
XLA Modules:
  0.0 537.9 jit_solution(7978137057800121709)
XLA Ops:
  7.3 2.9 stack.2
  10.1 5.0 all-to-all-start
  16.7 1.2 copy-done.2
  18.2 34.9 %all_gather.24 = bf16[256,1152]{0,1:T(8,128)(2,1)S(1)} all-gather(bf16[256,288]{0,1:T(8,128)(2,1)S(1)} %copy-done.5), channel_id=1, replica_groups=mesh['cfg'=2,'lat'=4,'seq'=16] {'lat'}, dimensions={1}, use_global_device_ids=true | all-gather | bytes 737280 | tf_op jit(solution)/shard_map/all_gather | solution.py:84
  53.2 2.8 fusion.31
  56.0 2.2 convolution_bitcast_fusion
  58.2 23.6 %all-gather = f32[16,576,6]{1,2,0:T(8,128)S(1)} all-gather(f32[1,576,6]{1,2,0:T(8,128)S(1)} %convolution_bitcast_fusion), channel_id=1, replica_groups=mesh['cfg'=2,'lat'=4,'seq'=16] {'seq'}, dimensions={0}, use_global_device_ids=true | all-gather | bytes 235008 | tf_op jit(solution)/shard_map/all_gather | solution.py:95
  83.1 8.3 %convolution_convert_fusion = bf16[384,3456]{1,0:T(8,128)(2,1)S(1)} fusion(bf16[384,1152]{1,0:T(8,128)(2,1)S(1)} %bitcast.58, bf16[1152,3456]{0,1:T(8,128)(2,1)} %all-gather.8.cloned.1.call-done), kind=kOutput, calls=%fused_computation.16 | convolution fusion | flops 3058974720 | bytes 11501568 | tf_op jit(solution)/shard_map/dot_general | solution.py:111
  91.4 1.5 fusion.60
  95.4 3.7 reshape.147
  99.0 95.5 %all-gather.10.cloned.1.call-done = bf16[6,1024,1152]{2,1,0:T(8,128)(2,1)} async-done(((bf16[6,64,1152]{2,1,0:T(8,128)(2,1)}), bf16[6,1024,1152]{2,1,0:T(8,128)(2,1)}) %all-gather.10.cloned.1.call-update) | async-done | bytes 14155792 | tf_op jit(solution)/shard_map/all_gather | solution.py:117
  194.6 18.7 %copy.28 = bf16[6,1024,1152]{1,2,0:T(8,128)(2,1)} copy(bf16[6,1024,1152]{2,1,0:T(8,128)(2,1)} %all-gather.10.cloned.1.call-done) | data formatting | bytes 28311552 | tf_op jit(solution)/shard_map/all_gather | solution.py:117
  213.3 81.1 %all-gather.12.cloned.1.call-done = bf16[6,1024,1152]{2,1,0:T(8,128)(2,1)} async-done(((bf16[6,64,1152]{2,1,0:T(8,128)(2,1)}), bf16[6,1024,1152]{2,1,0:T(8,128)(2,1)}) %all-gather.12.cloned.1.call-update) | async-done | bytes 14155792 | tf_op jit(solution)/shard_map/all_gather | solution.py:118
  294.4 18.7 %copy.30 = bf16[6,1024,1152]{1,2,0:T(8,128)(2,1)} copy(bf16[6,1024,1152]{2,1,0:T(8,128)(2,1)} %all-gather.12.cloned.1.call-done) | data formatting | bytes 28311552 | tf_op jit(solution)/shard_map/all_gather | solution.py:118
  313.1 18.5 %multiply_reduce_fusion = (f32[6,16,64]{2,1,0:T(8,128)S(1)}, f32[6,16,64,1024]{3,2,1,0:T(8,128)}) fusion(bf16[6,1024,16,72]{1,3,2,0:T(8,128)(2,1)} %bitcast.51, bf16[6,64,16,72]{3,2,1,0:T(8,128)(2,1)} %reshape.147), kind=kOutput, calls=%fused_computation.1 | convolution fusion | flops 918546432 | bytes 40230912 | tf_op jit(solution)/shard_map/lqhd,lkhd->lhqk/dot_general | solution.py:123
  331.6 11.2 %fusion = f32[6,16,64]{2,1,0:T(8,128)S(1)} fusion(f32[6,16,64,1024]{3,2,1,0:T(8,128)} %get-tuple-element.29, f32[6,16,64]{2,1,0:T(8,128)S(1)} %broadcast_maximum_fusion), kind=kLoop, calls=%fused_computation.2 | loop fusion | flops 18868224 | bytes 25214976 | tf_op jit(solution)/shard_map/reduce_sum | solution.py:128
  342.8 14.8 %fusion.20 = bf16[6,64,16,72]{3,1,2,0:T(8,128)(2,1)S(1)} fusion(bf16[6,1024,16,72]{1,3,2,0:T(8,128)(2,1)} %bitcast.52, f32[6,16,64,1024]{3,2,1,0:T(8,128)} %get-tuple-element.29, f32[6,16,64]{2,1,0:T(8,128)S(1)} %broadcast_maximum_fusion, f32[6,64,16]{1,2,0:T(8,128)S(1)} %bitcast.59), kind=kOutput, calls=%fused_computation.25 | convolution fusion | flops 925728768 | bytes 40255488 | tf_op jit(solution)/shard_map/lhqk,lkhd->lhqd/dot_general | solution.py:129
  357.6 2.2 copy.31
  359.8 3.2 convert_element_type.64
  363.1 3.3 fusion.62
  368.1 56.8 %all-gather.16.cloned.1.call-done = bf16[1152,4608]{0,1:T(8,128)(2,1)} async-done(((bf16[1152,288]{0,1:T(8,128)(2,1)}), bf16[1152,4608]{0,1:T(8,128)(2,1)}) %all-gather.16.cloned.1.call-update) | async-done | bytes 10616848 | tf_op jit(solution)/shard_map/all_gather | solution.py:146
  424.9 82.7 %all-gather.18.cloned.1.call-done = bf16[4608,1152]{1,0:T(8,128)(2,1)} async-done(((bf16[288,1152]{1,0:T(8,128)(2,1)}), bf16[4608,1152]{1,0:T(8,128)(2,1)}) %all-gather.18.cloned.1.call-update) | async-done | bytes 10616848 | tf_op jit(solution)/shard_map/all_gather | solution.py:147
  507.6 17.6 %fusion.14 = f32[384,1152]{1,0:T(8,128)} fusion(bf16[4608,1152]{1,0:T(8,128)(2,1)} %all-gather.18.cloned.1.call-done, bf16[384,1152]{1,0:T(8,128)(2,1)S(1)} %bitcast.57, bf16[1152,4608]{0,1:T(8,128)(2,1)} %all-gather.16.cloned.1.call-done), kind=kOutput, calls=%fused_computation.17 | convolution fusion | flops 8169652224 | bytes 23887872 | tf_op jit(solution)/shard_map/dot_general | solution.py:152
  525.3 2.5 fusion.59
  (68 shorter events, 10.6 us)
Async XLA Ops:
  6.5 49.5 %copy-start = (bf16[1001,1152]{1,0:T(8,128)(2,1)S(1)}, bf16[1001,1152]{1,0:T(8,128)(2,1)}, u32[]{:S(2)}) copy-start(bf16[1001,1152]{1,0:T(8,128)(2,1)} %param.23) | copy-start | bytes 6918916
  6.5 76.6 %all-gather.8.cloned.1.call-start = ((), (), s32[]{:S(2)}) async-start(), calls=%async_computation.1 | async-start | bytes 8460288 | tf_op jit(solution)/shard_map/all_gather | solution.py:107
  10.1 5.0 copy-start.11
  10.1 6.0 %copy-start.6 = (f32[6,64,16]{1,2,0:T(8,128)S(1)}, f32[6,64,16]{1,2,0:T(8,128)}, u32[]{:S(2)}) copy-start(f32[6,64,16]{1,2,0:T(8,128)} %param.16) | copy-start | bytes 73732
  10.1 6.0 %copy-start.7 = (bf16[16,1152]{1,0:T(8,128)(2,1)S(1)}, bf16[16,1152]{1,0:T(8,128)(2,1)}, u32[]{:S(2)}) copy-start(bf16[16,1152]{1,0:T(8,128)(2,1)} %param.22) | copy-start | bytes 110596
  10.1 43.1 %all-to-all-start = ((bf16[4,1152,288]{1,2,0:T(8,128)(2,1)}), bf16[4,1152,288]{1,2,0:T(8,128)(2,1)}, u32[]{:S(2)}, u32[]{:S(2)}) async-start(bf16[4,1152,288]{1,2,0:T(8,128)(2,1)} %stack.2), calls=%async_computation | async-start | bytes 5308416 | tf_op jit(solution)/shard_map/all_to_all | solution.py:86
  15.1 179.5 %all-gather.10.cloned.1.call-start = ((), (), s32[]{:S(2)}) async-start(), calls=%async_computation.2 | async-start | bytes 15040512 | tf_op jit(solution)/shard_map/all_gather | solution.py:117
  15.9 2.3 copy-start.5
  16.1 36.9 %copy-start.12 = (s32[6]{0:T(128)S(1)}, s32[6]{0:T(128)}, u32[]{:S(2)}) copy-start(s32[6]{0:T(128)} %param.18) | copy-start | bytes 76
  16.7 1.2 copy-start.2
  58.2 23.8 %copy-start.3 = (f32[6,64,1152]{2,1,0:T(8,128)S(1)}, f32[6,64,1152]{2,1,0:T(8,128)}, u32[]{:S(2)}) copy-start(f32[6,64,1152]{2,1,0:T(8,128)} %copy-done.2) | copy-start | bytes 5308420
  92.9 201.5 %all-gather.12.cloned.1.call-start = ((), (), s32[]{:S(2)}) async-start(), calls=%async_computation.3 | async-start | bytes 15040512 | tf_op jit(solution)/shard_map/all_gather | solution.py:118
  93.6 269.4 %all-gather.14.cloned.1.call-start = ((), (), s32[]{:S(2)}) async-start(), calls=%async_computation.4 | async-start | bytes 2820096 | tf_op jit(solution)/shard_map/all_gather | solution.py:108
  94.2 330.7 %all-gather.16.cloned.1.call-start = ((), (), s32[]{:S(2)}) async-start(), calls=%async_computation.5 | async-start | bytes 11280384 | tf_op jit(solution)/shard_map/all_gather | solution.py:146
  94.8 412.8 %all-gather.18.cloned.1.call-start = ((), (), s32[]{:S(2)}) async-start(), calls=%async_computation.6 | async-start | bytes 11280384 | tf_op jit(solution)/shard_map/all_gather | solution.py:147
  366.4 1.3 copy-start.4
  525.3 2.9 copy-start.10
  525.3 5.7 %copy-start.1 = (bf16[1001,1152]{1,0:T(8,128)(2,1)S(1)}, bf16[1001,1152]{1,0:T(8,128)(2,1)}, u32[]{:S(2)}) copy-start(bf16[1001,1152]{1,0:T(8,128)(2,1)} %param.23) | copy-start | bytes 6918916
  527.8 2.5 copy-start.8
  527.8 2.5 copy-start.9
  528.7 1.6 collective-permute-start
Sparse Core Ops, SparseCore 0:
  9.5 73.5 all-gather.7
  93.0 101.5 all-gather.9
  196.7 97.6 all-gather.11
  296.4 45.8 all-gather.13
  344.3 80.5 all-gather.15
  426.9 80.6 all-gather.17
